TPU v7x, 32 devices: a whole 2x2x4 slice. The times are simulated.
32 devices in a mesh: seg: 2 (over y), row: 8 (over z, x), col: 2 (over core).
Axes of the slice: x: 2, y: 2, z: 4, core: 2. Of those that a mesh axis runs over, the one named last changes fastest.
Arguments:
- slices: bfloat16 [4, 4096, 4096], P('col', 'seg', 'row'), may hold values from -1 to 1
Outputs:
- prefixes: bfloat16 [4, 4096, 4096], P('col', 'seg', 'row')
All inputs are finite; a program needn't handle non-finite values.
Results may differ from a plain program's by a relative error of at most 0.004.
Values may be sent and summed in bfloat16 or wider, within the bound.
No kernel may reach another device: no remote copies, remote signals or barrier semaphores. Data moves between devices by JAX's collectives and lax.ppermute only.
A program may use at most 128 MiB of HBM per device.

v0:
```python
import math
import jax
import jax.numpy as jnp
from jax import lax
from jax.sharding import PartitionSpec as P

ORDER = 4096


def passed_along(value, axis, by):
    count = lax.axis_size(axis)
    pairs = [(i, i + by) for i in range(count) if 0 <= i + by < count]
    return lax.ppermute(value, axis, pairs)


def column_panel(tile):
    return lax.all_gather(tile, "seg", axis=0, tiled=True)


def times_panel(left_tile, right_block):
    gathered = lax.all_gather(left_tile, "row", axis=1, tiled=True)
    return jnp.dot(gathered, right_block, preferred_element_type=jnp.float32)


def earlier_panel(tile, distance):
    return passed_along(column_panel(tile), "col", distance)


def local(slices):
    group_index = lax.axis_index("col")
    group_count = lax.axis_size("col")
    history = [slices[0]]
    history.append(times_panel(slices[1], column_panel(history[-1])).astype(jnp.bfloat16))
    running = history[-1]
    distance = 1
    while distance < group_count:
        product = times_panel(running, earlier_panel(running, distance)).astype(jnp.bfloat16)
        running = jnp.where(group_index >= distance, product, running)
        distance = distance * 2
    carried_block = earlier_panel(running, 1)
    factor = math.sqrt(ORDER)
    results = []
    for local_tile in history:
        applied = times_panel(local_tile, carried_block)
        chosen = jnp.where(group_index > 0, applied, local_tile.astype(jnp.float32))
        results.append((chosen * factor).astype(jnp.bfloat16))
    return jnp.stack(results, axis=0)


def solution(mesh):
    in_specs = (P("col", "seg", "row"),)
    out_specs = P("col", "seg", "row")
    return jax.shard_map(local, mesh=mesh, in_specs=in_specs, out_specs=out_specs, check_vma=False)
```

profile of v0, /device:TPU:0, one launch (start us, length us, event | category | flops | bytes accessed | tf_op | source)
XLA Modules:
  0.0 920.9 jit_solution(10815625901203171808)
XLA Ops:
  6.5 4.5 fusion.19
  11.1 0.0 all-gather.16.cloned.1.call-start
  11.2 0.7 all-gather.16.cloned.1.call-update
  11.9 0.0 all-gather.12.cloned.1.call-start
  11.9 58.8 %all-gather.18.cloned.1.call-done = bf16[1,4096,512]{2,1,0:T(8,128)(2,1)} async-done(((bf16[1,2048,512]{2,1,0:T(8,128)(2,1)}), bf16[1,4096,512]{2,1,0:T(8,128)(2,1)}) %all-gather.18.cloned.1.call-update) | async-done | bytes 4194320 | tf_op jit(solution)/shard_map/all_gather | solution.py:17
  70.7 229.4 %all-gather.16.cloned.1.call-done = bf16[1,2048,4096]{2,1,0:T(8,128)(2,1)} async-done(((bf16[1,2048,512]{2,1,0:T(8,128)(2,1)}), bf16[1,2048,4096]{2,1,0:T(8,128)(2,1)}) %all-gather.16.cloned.1.call-update) | async-done | bytes 16777232 | tf_op jit(solution)/shard_map/all_gather | solution.py:21
  300.1 14.5 %fusion.9 = bf16[2048,512]{1,0:T(8,128)(2,1)} fusion(bf16[1,4096,512]{2,1,0:T(8,128)(2,1)} %all-gather.18.cloned.1.call-done, bf16[1,2048,4096]{2,1,0:T(8,128)(2,1)} %all-gather.16.cloned.1.call-done), kind=kOutput, calls=%fused_computation.10 | convolution fusion | flops 8590983168 | bytes 23068672 | tf_op jit(solution)/shard_map/dot_general | solution.py:22
  314.6 0.0 all-gather.10.cloned.1.call-start
  314.7 0.5 all-gather.10.cloned.1.call-update
  315.2 0.0 all-gather.14.cloned.1.call-start
  315.3 54.4 %all-gather.12.cloned.1.call-done = bf16[4096,512]{1,0:T(8,128)(2,1)} async-done(((bf16[2048,512]{1,0:T(8,128)(2,1)}), bf16[4096,512]{1,0:T(8,128)(2,1)}) %all-gather.12.cloned.1.call-update) | async-done | bytes 4194320 | tf_op jit(solution)/shard_map/all_gather | solution.py:17
  369.7 3.6 collective-permute-start
  373.3 5.1 collective-permute-done
  378.4 220.5 %all-gather.10.cloned.1.call-done = bf16[2048,4096]{1,0:T(8,128)(2,1)} async-done(((bf16[2048,512]{1,0:T(8,128)(2,1)}), bf16[2048,4096]{1,0:T(8,128)(2,1)}) %all-gather.10.cloned.1.call-update) | async-done | bytes 16777232 | tf_op jit(solution)/shard_map/all_gather | solution.py:21
  598.9 14.5 %fusion.18 = bf16[2048,512]{1,0:T(8,128)(2,1)} fusion(bf16[2048,512]{1,0:T(8,128)(2,1)S(1)} %copy-done, bf16[2048,4096]{1,0:T(8,128)(2,1)} %all-gather.10.cloned.1.call-done, bf16[4096,512]{1,0:T(8,128)(2,1)} %collective-permute-done, pred[]{:T(512)S(6)} %ge.3), kind=kOutput, calls=%fused_computation.14 | convolution fusion | flops 8592031744 | bytes 25165824 | tf_op jit(solution)/shard_map/dot_general | solution.py:22
  613.5 0.0 all-gather.20.cloned.1.call-start
  613.5 0.5 all-gather.20.cloned.1.call-update
  614.1 54.5 %all-gather.14.cloned.1.call-done = bf16[4096,512]{1,0:T(8,128)(2,1)} async-done(((bf16[2048,512]{1,0:T(8,128)(2,1)}), bf16[4096,512]{1,0:T(8,128)(2,1)}) %all-gather.14.cloned.1.call-update) | async-done | bytes 4194320 | tf_op jit(solution)/shard_map/all_gather | solution.py:17
  668.6 3.6 collective-permute-start.1
  672.2 5.0 collective-permute-done.1
  677.2 15.9 %fusion.14 = bf16[1,2048,512]{2,1,0:T(8,128)(2,1)} fusion(bf16[2048,512]{1,0:T(8,128)(2,1)S(1)} %copy-done, bf16[2048,4096]{1,0:T(8,128)(2,1)} %all-gather.10.cloned.1.call-done, bf16[4096,512]{1,0:T(8,128)(2,1)} %collective-permute-done.1, pred[]{:T(512)S(6)} %gt.4), kind=kOutput, calls=%fused_computation.12 | convolution fusion | flops 8594128896 | bytes 25165824 | tf_op jit(solution)/shard_map/dot_general | solution.py:22
  693.1 204.6 %all-gather.20.cloned.1.call-done = bf16[1,2048,4096]{2,1,0:T(8,128)(2,1)} async-done(((bf16[1,2048,512]{2,1,0:T(8,128)(2,1)}), bf16[1,2048,4096]{2,1,0:T(8,128)(2,1)}) %all-gather.20.cloned.1.call-update) | async-done | bytes 16777232 | tf_op jit(solution)/shard_map/all_gather | solution.py:21
  897.8 13.9 %fusion.15 = bf16[1,2048,512]{2,1,0:T(8,128)(2,1)S(1)} fusion(bf16[4096,512]{1,0:T(8,128)(2,1)} %collective-permute-done.1, bf16[1,2048,4096]{2,1,0:T(8,128)(2,1)} %all-gather.20.cloned.1.call-done, pred[]{:T(512)S(6)} %gt.4, bf16[2,2048,512]{2,1,0:T(8,128)(2,1)} %param.1), kind=kOutput, calls=%fused_computation.13 | convolution fusion | flops 8594128896 | bytes 25165824 | tf_op jit(solution)/shard_map/dot_general | solution.py:22
  911.7 2.4 pad_maximum_fusion
  (8 shorter events, 0.1 us)
Async XLA Ops:
  6.5 64.2 %all-gather.18.cloned.1.call-start = ((), (), s32[]{:S(2)}) async-start(), calls=%async_computation.4 | async-start | bytes 6291456 | tf_op jit(solution)/shard_map/all_gather | solution.py:17
  11.1 289.0 %all-gather.16.cloned.1.call-start = ((), (), s32[]{:S(2)}) async-start(), calls=%async_computation.3 | async-start | bytes 18874368 | tf_op jit(solution)/shard_map/all_gather | solution.py:21
  11.9 357.8 %all-gather.12.cloned.1.call-start = ((), (), s32[]{:S(2)}) async-start(), calls=%async_computation.1 | async-start | bytes 6291456 | tf_op jit(solution)/shard_map/all_gather | solution.py:17
  314.6 284.3 %copy-start = (bf16[2048,512]{1,0:T(8,128)(2,1)S(1)}, bf16[2048,512]{1,0:T(8,128)(2,1)}, u32[]{:S(2)}) copy-start(bf16[2048,512]{1,0:T(8,128)(2,1)} %fusion.9) | copy-start | bytes 6291460
  314.6 284.3 %all-gather.10.cloned.1.call-start = ((), (), s32[]{:S(2)}) async-start(), calls=%async_computation | async-start | bytes 18874368 | tf_op jit(solution)/shard_map/all_gather | solution.py:21
  315.2 353.3 %all-gather.14.cloned.1.call-start = ((), (), s32[]{:S(2)}) async-start(), calls=%async_computation.2 | async-start | bytes 6291456 | tf_op jit(solution)/shard_map/all_gather | solution.py:17
  369.7 8.7 collective-permute-start
  613.5 284.3 %all-gather.20.cloned.1.call-start = ((), (), s32[]{:S(2)}) async-start(), calls=%async_computation.5 | async-start | bytes 18874368 | tf_op jit(solution)/shard_map/all_gather | solution.py:21
  668.6 8.7 collective-permute-start.1
  693.1 218.5 %copy-start.1 = (bf16[1,2048,512]{2,1,0:T(8,128)(2,1)S(1)}, bf16[1,2048,512]{2,1,0:T(8,128)(2,1)}, u32[]{:S(2)}) copy-start(bf16[1,2048,512]{2,1,0:T(8,128)(2,1)} %fusion.14) | copy-start | bytes 6291460
Sparse Core Ops, SparseCore 0:
  11.2 59.4 all-gather.17
  72.8 227.2 all-gather.15
  314.8 54.8 all-gather.11
  371.6 227.2 all-gather.9
  613.6 54.9 all-gather.13
  670.5 227.2 all-gather.19
where the time goes:
time: 921 us
  waiting for transfers between devices  834 us (91%)
  matrix products  58.8 us (6%)
  between operations  13.5 us (1%)
    all_gather x3, waiting for transfers between devices, times_panel(): gathered = lax.all_gather(left_tile, 'row', axis=1, tiled=True)  655 us
    all_gather x3, waiting for transfers between devices, column_panel(): return lax.all_gather(tile, 'seg', axis=0, tiled=True)  168 us
    dot_general x4, matrix products, times_panel(): return jnp.dot(gathered, right_block, preferred_element_type=jnp.float32)  58.8 us
  transfers between devices with their start and end apart: 8, of which 8 were waited for; matrix products, arithmetic and copies ran while one was open for 2% of the time, Pallas kernels for 0%

commit v1 on v0

--- a/solution.py
+++ b/solution.py
@@ -18,7 +18,12 @@
 
 
 def times_panel(left_tile, right_block):
-    gathered = lax.all_gather(left_tile, "row", axis=1, tiled=True)
+    ring = [left_tile]
+    for hop in range(7):
+        ring.append(lax.ppermute(ring[-1], "row", [(dev, (dev + 1) % 8) for dev in range(8)]))
+    gathered = jnp.roll(
+        jnp.concatenate(ring[::-1], axis=1), (lax.axis_index("row") + 1) * ring[0].shape[1], axis=1
+    )
     return jnp.dot(gathered, right_block, preferred_element_type=jnp.float32)
 
 

time: 921 us -> 1090 us (1.18)
  waiting for transfers between devices: 834 us -> 925 us
  local copies, waits for them, and re-layouts: 4.55 us -> 73.9 us
    ppermute x0 -> x21, waiting for transfers between devices: none -> 925 us  [times_panel(): lax.ppermute(ring[-1], 'row', [(dev, (dev + 1) % 8) for dev in range(8)])]
    all_gather x3 -> x0, waiting for transfers between devices: 655 us -> none  [times_panel(): gathered = lax.all_gather(left_tile, 'row', axis=1, tiled=True)]
    all_gather x3, waiting for transfers between devices: 168 us -> 0.01 us  [column_panel(): return lax.all_gather(tile, 'seg', axis=0, tiled=True)]
    unnamed x4 -> x58, local copies, waits for them, and re-layouts: 0.01 us -> 61.9 us
  transfers between devices with their start and end apart: 8 -> 26, of which waited for: 8 -> 21; matrix products, arithmetic and copies ran while one was open for 2% -> 6% of each run, Pallas kernels for 0% -> 0%
where the time goes in v1:
time: 1090 us
  waiting for transfers between devices  925 us (85%)
  local copies, waits for them, and re-layouts  73.9 us (7%)
  matrix products  61.3 us (6%)
  between operations  13.3 us (1%)
  starting transfers between devices  12.6 us (1%)
    ppermute x21, waiting for transfers between devices, times_panel(): lax.ppermute(ring[-1], 'row', [(dev, (dev + 1) % 8) for dev in range(8)])  925 us
    unnamed x58, local copies, waits for them, and re-layouts  61.9 us
    dot_general x4, matrix products, times_panel(): return jnp.dot(gathered, right_block, preferred_element_type=jnp.float32)  61.3 us
  transfers between devices with their start and end apart: 26, of which 21 were waited for; matrix products, arithmetic and copies ran while one was open for 6% of the time, Pallas kernels for 0%

profile of v1, /device:TPU:0, one launch (start us, length us, event | category | flops | bytes accessed | tf_op | source)
XLA Modules:
  0.0 1090.8 jit_solution(268260025311292911)
XLA Ops:
  12.1 48.7 %collective-permute-done.7 = bf16[2048,512]{1,0:T(8,128)(2,1)S(1)} collective-permute-done((bf16[2048,512]{1,0:T(8,128)(2,1)S(1)}, bf16[2048,512]{1,0:T(8,128)(2,1)S(1)}, u32[]{:S(2)}, u32[]{:S(2)}) %collective-permute-start.7) | collective-permute-done | bytes 2097184 | tf_op jit(solution)/shard_map/ppermute | solution.py:23
  62.1 49.5 %collective-permute-done.8 = bf16[2048,512]{1,0:T(8,128)(2,1)S(1)} collective-permute-done((bf16[2048,512]{1,0:T(8,128)(2,1)S(1)}, bf16[2048,512]{1,0:T(8,128)(2,1)S(1)}, u32[]{:S(2)}, u32[]{:S(2)}) %collective-permute-start.8) | collective-permute-done | bytes 2097184 | tf_op jit(solution)/shard_map/ppermute | solution.py:23
  113.0 48.6 %collective-permute-done.9 = bf16[2048,512]{1,0:T(8,128)(2,1)S(1)} collective-permute-done((bf16[2048,512]{1,0:T(8,128)(2,1)S(1)}, bf16[2048,512]{1,0:T(8,128)(2,1)S(1)}, u32[]{:S(2)}, u32[]{:S(2)}) %collective-permute-start.9) | collective-permute-done | bytes 2097184 | tf_op jit(solution)/shard_map/ppermute | solution.py:23
  162.9 47.8 %collective-permute-done.10 = bf16[2048,512]{1,0:T(8,128)(2,1)S(1)} collective-permute-done((bf16[2048,512]{1,0:T(8,128)(2,1)S(1)}, bf16[2048,512]{1,0:T(8,128)(2,1)S(1)}, u32[]{:S(2)}, u32[]{:S(2)}) %collective-permute-start.10) | collective-permute-done | bytes 2097184 | tf_op jit(solution)/shard_map/ppermute | solution.py:23
  212.1 46.9 %collective-permute-done.11 = bf16[2048,512]{1,0:T(8,128)(2,1)S(1)} collective-permute-done((bf16[2048,512]{1,0:T(8,128)(2,1)S(1)}, bf16[2048,512]{1,0:T(8,128)(2,1)S(1)}, u32[]{:S(2)}, u32[]{:S(2)}) %collective-permute-start.11) | collective-permute-done | bytes 2097184 | tf_op jit(solution)/shard_map/ppermute | solution.py:23
  260.3 46.2 %collective-permute-done.12 = bf16[2048,512]{1,0:T(8,128)(2,1)} collective-permute-done((bf16[2048,512]{1,0:T(8,128)(2,1)S(1)}, bf16[2048,512]{1,0:T(8,128)(2,1)}, u32[]{:S(2)}, u32[]{:S(2)}) %collective-permute-start.12) | collective-permute-done | bytes 2097184 | tf_op jit(solution)/shard_map/ppermute | solution.py:23
  309.0 43.0 %collective-permute-done.13 = bf16[2048,512]{1,0:T(8,128)(2,1)} collective-permute-done((bf16[2048,512]{1,0:T(8,128)(2,1)}, bf16[2048,512]{1,0:T(8,128)(2,1)}, u32[]{:S(2)}, u32[]{:S(2)}) %collective-permute-start.13) | collective-permute-done | bytes 2097184 | tf_op jit(solution)/shard_map/ppermute | solution.py:23
  370.6 15.0 %fusion.8 = bf16[2048,512]{0,1:T(8,128)(2,1)} fusion(bf16[1,4096,512]{1,2,0:T(8,128)(2,1)} %all-gather.9.cloned.1.call-done, s32[]{:T(128)S(6)} %select_n.40, bf16[2048,4096]{1,0:T(8,128)(2,1)} %constant_dynamic-update-slice_fusion), kind=kOutput, calls=%fused_computation.15 | convolution fusion | flops 8624537600 | bytes 23068676 | tf_op jit(solution)/shard_map/dot_general | solution.py:27
  385.6 45.7 %collective-permute-done.14 = bf16[2048,512]{0,1:T(8,128)(2,1)S(1)} collective-permute-done((bf16[2048,512]{0,1:T(8,128)(2,1)}, bf16[2048,512]{0,1:T(8,128)(2,1)S(1)}, u32[]{:S(2)}, u32[]{:S(2)}) %collective-permute-start.14) | collective-permute-done | bytes 2097184 | tf_op jit(solution)/shard_map/ppermute | solution.py:23
  431.3 45.9 %collective-permute-done.15 = bf16[2048,512]{0,1:T(8,128)(2,1)S(1)} collective-permute-done((bf16[2048,512]{0,1:T(8,128)(2,1)S(1)}, bf16[2048,512]{0,1:T(8,128)(2,1)S(1)}, u32[]{:S(2)}, u32[]{:S(2)}) %collective-permute-start.15) | collective-permute-done | bytes 2097184 | tf_op jit(solution)/shard_map/ppermute | solution.py:23
  479.7 48.7 %collective-permute-done.16 = bf16[2048,512]{0,1:T(8,128)(2,1)S(1)} collective-permute-done((bf16[2048,512]{0,1:T(8,128)(2,1)S(1)}, bf16[2048,512]{0,1:T(8,128)(2,1)S(1)}, u32[]{:S(2)}, u32[]{:S(2)}) %collective-permute-start.16) | collective-permute-done | bytes 2097184 | tf_op jit(solution)/shard_map/ppermute | solution.py:23
  528.4 45.0 %collective-permute-done = bf16[2048,512]{0,1:T(8,128)(2,1)} collective-permute-done((bf16[2048,512]{0,1:T(8,128)(2,1)S(1)}, bf16[2048,512]{0,1:T(8,128)(2,1)}, u32[]{:S(2)}, u32[]{:S(2)}) %collective-permute-start) | collective-permute-done | bytes 2097184 | tf_op jit(solution)/shard_map/ppermute | solution.py:23
  573.4 44.9 %collective-permute-done.17 = bf16[2048,512]{0,1:T(8,128)(2,1)} collective-permute-done((bf16[2048,512]{0,1:T(8,128)(2,1)S(1)}, bf16[2048,512]{0,1:T(8,128)(2,1)}, u32[]{:S(2)}, u32[]{:S(2)}) %collective-permute-start.17) | collective-permute-done | bytes 2097184 | tf_op jit(solution)/shard_map/ppermute | solution.py:23
  618.4 44.9 %collective-permute-done.1 = bf16[2048,512]{0,1:T(8,128)(2,1)} collective-permute-done((bf16[2048,512]{0,1:T(8,128)(2,1)}, bf16[2048,512]{0,1:T(8,128)(2,1)}, u32[]{:S(2)}, u32[]{:S(2)}) %collective-permute-start.1) | collective-permute-done | bytes 2097184 | tf_op jit(solution)/shard_map/ppermute | solution.py:23
  663.3 44.9 %collective-permute-done.18 = bf16[2048,512]{0,1:T(8,128)(2,1)} collective-permute-done((bf16[2048,512]{0,1:T(8,128)(2,1)}, bf16[2048,512]{0,1:T(8,128)(2,1)}, u32[]{:S(2)}, u32[]{:S(2)}) %collective-permute-start.18) | collective-permute-done | bytes 2097184 | tf_op jit(solution)/shard_map/ppermute | solution.py:23
  708.2 44.9 %collective-permute-done.2 = bf16[2048,512]{0,1:T(8,128)(2,1)} collective-permute-done((bf16[2048,512]{0,1:T(8,128)(2,1)}, bf16[2048,512]{0,1:T(8,128)(2,1)}, u32[]{:S(2)}, u32[]{:S(2)}) %collective-permute-start.2) | collective-permute-done | bytes 2097184 | tf_op jit(solution)/shard_map/ppermute | solution.py:23
  753.2 44.9 %collective-permute-done.19 = bf16[2048,512]{0,1:T(8,128)(2,1)} collective-permute-done((bf16[2048,512]{0,1:T(8,128)(2,1)}, bf16[2048,512]{0,1:T(8,128)(2,1)}, u32[]{:S(2)}, u32[]{:S(2)}) %collective-permute-start.19) | collective-permute-done | bytes 2097184 | tf_op jit(solution)/shard_map/ppermute | solution.py:23
  801.4 41.6 %collective-permute-done.3 = bf16[2048,512]{0,1:T(8,128)(2,1)} collective-permute-done((bf16[2048,512]{0,1:T(8,128)(2,1)}, bf16[2048,512]{0,1:T(8,128)(2,1)}, u32[]{:S(2)}, u32[]{:S(2)}) %collective-permute-start.3) | collective-permute-done | bytes 2097184 | tf_op jit(solution)/shard_map/ppermute | solution.py:23
  843.1 44.9 %collective-permute-done.20 = bf16[2048,512]{0,1:T(8,128)(2,1)} collective-permute-done((bf16[2048,512]{0,1:T(8,128)(2,1)}, bf16[2048,512]{0,1:T(8,128)(2,1)}, u32[]{:S(2)}, u32[]{:S(2)}) %collective-permute-start.20) | collective-permute-done | bytes 2097184 | tf_op jit(solution)/shard_map/ppermute | solution.py:23
  901.7 15.4 %fusion.19 = bf16[2048,512]{0,1:T(8,128)(2,1)} fusion(bf16[2048,512]{0,1:T(8,128)(2,1)} %fusion.8, bf16[4096,512]{0,1:T(8,128)(2,1)} %collective-permute-done.21, pred[]{:T(512)S(6)} %ge.3, s32[]{:T(128)S(6)} %select_n.40, bf16[2048,4096]{0,1:T(8,128)(2,1)} %copy-done.17), kind=kOutput, calls=%fused_computation.19 | convolution fusion | flops 8625586176 | bytes 25165828 | tf_op jit(solution)/shard_map/dot_general | solution.py:27
  927.3 46.0 %collective-permute-done.5 = bf16[2048,512]{0,1:T(8,128)(2,1)} collective-permute-done((bf16[2048,512]{0,1:T(8,128)(2,1)}, bf16[2048,512]{0,1:T(8,128)(2,1)}, u32[]{:S(2)}, u32[]{:S(2)}) %collective-permute-start.5) | collective-permute-done | bytes 2097184 | tf_op jit(solution)/shard_map/ppermute | solution.py:23
  976.6 42.0 %collective-permute-done.6 = bf16[2048,512]{0,1:T(8,128)(2,1)} collective-permute-done((bf16[2048,512]{0,1:T(8,128)(2,1)}, bf16[2048,512]{0,1:T(8,128)(2,1)}, u32[]{:S(2)}, u32[]{:S(2)}) %collective-permute-start.6) | collective-permute-done | bytes 2097184 | tf_op jit(solution)/shard_map/ppermute | solution.py:23
  1042.6 15.6 %fusion.18 = bf16[1,2048,512]{1,2,0:T(8,128)(2,1)} fusion(bf16[2048,512]{0,1:T(8,128)(2,1)} %fusion.8, bf16[4096,512]{0,1:T(8,128)(2,1)} %collective-permute-done.22, pred[]{:T(512)S(6)} %gt.4, s32[]{:T(128)S(6)} %select_n.40, bf16[2048,4096]{0,1:T(8,128)(2,1)} %copy-done.17), kind=kOutput, calls=%fused_computation.18 | convolution fusion | flops 8627683328 | bytes 25165828 | tf_op jit(solution)/shard_map/dot_general | solution.py:27
  1058.2 15.3 %fusion.15 = bf16[1,2048,512]{1,2,0:T(8,128)(2,1)} fusion(bf16[4096,512]{0,1:T(8,128)(2,1)} %collective-permute-done.22, s32[]{:T(128)S(6)} %select_n.40, bf16[2048,4096]{0,1:T(8,128)(2,1)} %constant_dynamic-update-slice_fusion.16, pred[]{:T(512)S(6)} %gt.4, bf16[1,2048,512]{1,2,0:T(8,128)(2,1)S(1)} %copy-done), kind=kOutput, calls=%fused_computation.17 | convolution fusion | flops 8627683328 | bytes 25165828 | tf_op jit(solution)/shard_map/dot_general | solution.py:27
  (99 shorter events, 101.0 us)
Async XLA Ops:
  6.5 364.0 %all-gather.9.cloned.1.call-start = ((), (), s32[]{:S(2)}) async-start(), calls=%async_computation.2 | async-start | bytes 6291456 | tf_op jit(solution)/shard_map/all_gather | solution.py:17
  9.0 51.7 %collective-permute-start.7 = (bf16[2048,512]{1,0:T(8,128)(2,1)S(1)}, bf16[2048,512]{1,0:T(8,128)(2,1)S(1)}, u32[]{:S(2)}, u32[]{:S(2)}) collective-permute-start(bf16[2048,512]{1,0:T(8,128)(2,1)S(1)} %get-tuple-element.6), channel_id=1, source_target_pairs={{0,2},{2,4},{4,6},{6,8},{8,10},{10,12},{12,14},{14,0},{1,3},{3,5},... | collective-permute-start | bytes 6291464 | tf_op jit(solution)/shard_map/ppermute | solution.py:23
  62.1 49.5 %collective-permute-start.8 = (bf16[2048,512]{1,0:T(8,128)(2,1)S(1)}, bf16[2048,512]{1,0:T(8,128)(2,1)S(1)}, u32[]{:S(2)}, u32[]{:S(2)}) collective-permute-start(bf16[2048,512]{1,0:T(8,128)(2,1)S(1)} %collective-permute-done.7), channel_id=1, source_target_pairs={{0,2},{2,4},{4,6},{6,8},{8,10},{10,12},{12,14},{14,0},{1,3},{3,5},... | collective-permute-start | bytes 6291464 | tf_op jit(solution)/shard_map/ppermute | solution.py:23
  113.0 48.6 %collective-permute-start.9 = (bf16[2048,512]{1,0:T(8,128)(2,1)S(1)}, bf16[2048,512]{1,0:T(8,128)(2,1)S(1)}, u32[]{:S(2)}, u32[]{:S(2)}) collective-permute-start(bf16[2048,512]{1,0:T(8,128)(2,1)S(1)} %collective-permute-done.8), channel_id=1, source_target_pairs={{0,2},{2,4},{4,6},{6,8},{8,10},{10,12},{12,14},{14,0},{1,3},{3,5},... | collective-permute-start | bytes 6291464 | tf_op jit(solution)/shard_map/ppermute | solution.py:23
  162.9 47.8 %collective-permute-start.10 = (bf16[2048,512]{1,0:T(8,128)(2,1)S(1)}, bf16[2048,512]{1,0:T(8,128)(2,1)S(1)}, u32[]{:S(2)}, u32[]{:S(2)}) collective-permute-start(bf16[2048,512]{1,0:T(8,128)(2,1)S(1)} %collective-permute-done.9), channel_id=1, source_target_pairs={{0,2},{2,4},{4,6},{6,8},{8,10},{10,12},{12,14},{14,0},{1,3},{3,5},... | collective-permute-start | bytes 6291464 | tf_op jit(solution)/shard_map/ppermute | solution.py:23
  212.1 46.9 %collective-permute-start.11 = (bf16[2048,512]{1,0:T(8,128)(2,1)S(1)}, bf16[2048,512]{1,0:T(8,128)(2,1)S(1)}, u32[]{:S(2)}, u32[]{:S(2)}) collective-permute-start(bf16[2048,512]{1,0:T(8,128)(2,1)S(1)} %collective-permute-done.10), channel_id=1, source_target_pairs={{0,2},{2,4},{4,6},{6,8},{8,10},{10,12},{12,14},{14,0},{1,3},{3,5},... | collective-permute-start | bytes 6291464 | tf_op jit(solution)/shard_map/ppermute | solution.py:23
  260.3 46.2 %collective-permute-start.12 = (bf16[2048,512]{1,0:T(8,128)(2,1)S(1)}, bf16[2048,512]{1,0:T(8,128)(2,1)}, u32[]{:S(2)}, u32[]{:S(2)}) collective-permute-start(bf16[2048,512]{1,0:T(8,128)(2,1)S(1)} %collective-permute-done.11), channel_id=1, source_target_pairs={{0,2},{2,4},{4,6},{6,8},{8,10},{10,12},{12,14},{14,0},{1,3},{3,5},... | collective-permute-start | bytes 6291464 | tf_op jit(solution)/shard_map/ppermute | solution.py:23
  308.9 489.2 %all-gather.5.cloned.1.call-start = ((), (), s32[]{:S(2)}) async-start(), calls=%async_computation | async-start | bytes 6291456 | tf_op jit(solution)/shard_map/all_gather | solution.py:17
  385.6 45.7 %collective-permute-start.14 = (bf16[2048,512]{0,1:T(8,128)(2,1)}, bf16[2048,512]{0,1:T(8,128)(2,1)S(1)}, u32[]{:S(2)}, u32[]{:S(2)}) collective-permute-start(bf16[2048,512]{0,1:T(8,128)(2,1)} %fusion.8), channel_id=1, source_target_pairs={{0,2},{2,4},{4,6},{6,8},{8,10},{10,12},{12,14},{14,0},{1,3},{3,5},... | collective-permute-start | bytes 6291464 | tf_op jit(solution)/shard_map/ppermute | solution.py:23
  431.3 45.9 %collective-permute-start.15 = (bf16[2048,512]{0,1:T(8,128)(2,1)S(1)}, bf16[2048,512]{0,1:T(8,128)(2,1)S(1)}, u32[]{:S(2)}, u32[]{:S(2)}) collective-permute-start(bf16[2048,512]{0,1:T(8,128)(2,1)S(1)} %collective-permute-done.14), channel_id=1, source_target_pairs={{0,2},{2,4},{4,6},{6,8},{8,10},{10,12},{12,14},{14,0},{1,3},{3,5},... | collective-permute-start | bytes 6291464 | tf_op jit(solution)/shard_map/ppermute | solution.py:23
  477.2 51.2 %collective-permute-start.16 = (bf16[2048,512]{0,1:T(8,128)(2,1)S(1)}, bf16[2048,512]{0,1:T(8,128)(2,1)S(1)}, u32[]{:S(2)}, u32[]{:S(2)}) collective-permute-start(bf16[2048,512]{0,1:T(8,128)(2,1)S(1)} %collective-permute-done.15), channel_id=1, source_target_pairs={{0,2},{2,4},{4,6},{6,8},{8,10},{10,12},{12,14},{14,0},{1,3},{3,5},... | collective-permute-start | bytes 6291464 | tf_op jit(solution)/shard_map/ppermute | solution.py:23
  477.2 96.2 %collective-permute-start = (bf16[2048,512]{0,1:T(8,128)(2,1)S(1)}, bf16[2048,512]{0,1:T(8,128)(2,1)}, u32[]{:S(2)}, u32[]{:S(2)}) collective-permute-start(bf16[2048,512]{0,1:T(8,128)(2,1)S(1)} %bitcast.19), channel_id=1, source_target_pairs={{0,2},{2,4},{4,6},{6,8},{8,10},{10,12},{12,14},{14,0},{1,3},{3,5},... | collective-permute-start | bytes 6291464 | tf_op jit(solution)/shard_map/ppermute | solution.py:23
  528.4 90.0 %collective-permute-start.17 = (bf16[2048,512]{0,1:T(8,128)(2,1)S(1)}, bf16[2048,512]{0,1:T(8,128)(2,1)}, u32[]{:S(2)}, u32[]{:S(2)}) collective-permute-start(bf16[2048,512]{0,1:T(8,128)(2,1)S(1)} %collective-permute-done.16), channel_id=1, source_target_pairs={{0,2},{2,4},{4,6},{6,8},{8,10},{10,12},{12,14},{14,0},{1,3},{3,5},... | collective-permute-start | bytes 6291464 | tf_op jit(solution)/shard_map/ppermute | solution.py:23
  573.4 89.9 %collective-permute-start.1 = (bf16[2048,512]{0,1:T(8,128)(2,1)}, bf16[2048,512]{0,1:T(8,128)(2,1)}, u32[]{:S(2)}, u32[]{:S(2)}) collective-permute-start(bf16[2048,512]{0,1:T(8,128)(2,1)} %collective-permute-done), channel_id=1, source_target_pairs={{0,2},{2,4},{4,6},{6,8},{8,10},{10,12},{12,14},{14,0},{1,3},{3,5},... | collective-permute-start | bytes 6291464 | tf_op jit(solution)/shard_map/ppermute | solution.py:23
  618.3 89.9 %collective-permute-start.18 = (bf16[2048,512]{0,1:T(8,128)(2,1)}, bf16[2048,512]{0,1:T(8,128)(2,1)}, u32[]{:S(2)}, u32[]{:S(2)}) collective-permute-start(bf16[2048,512]{0,1:T(8,128)(2,1)} %collective-permute-done.17), channel_id=1, source_target_pairs={{0,2},{2,4},{4,6},{6,8},{8,10},{10,12},{12,14},{14,0},{1,3},{3,5},... | collective-permute-start | bytes 6291464 | tf_op jit(solution)/shard_map/ppermute | solution.py:23
  618.4 354.9 %all-gather.7.cloned.1.call-start = ((), (), s32[]{:S(2)}) async-start(), calls=%async_computation.1 | async-start | bytes 6291456 | tf_op jit(solution)/shard_map/all_gather | solution.py:17
  663.3 89.9 %collective-permute-start.2 = (bf16[2048,512]{0,1:T(8,128)(2,1)}, bf16[2048,512]{0,1:T(8,128)(2,1)}, u32[]{:S(2)}, u32[]{:S(2)}) collective-permute-start(bf16[2048,512]{0,1:T(8,128)(2,1)} %collective-permute-done.1), channel_id=1, source_target_pairs={{0,2},{2,4},{4,6},{6,8},{8,10},{10,12},{12,14},{14,0},{1,3},{3,5},... | collective-permute-start | bytes 6291464 | tf_op jit(solution)/shard_map/ppermute | solution.py:23
  708.2 89.9 %collective-permute-start.19 = (bf16[2048,512]{0,1:T(8,128)(2,1)}, bf16[2048,512]{0,1:T(8,128)(2,1)}, u32[]{:S(2)}, u32[]{:S(2)}) collective-permute-start(bf16[2048,512]{0,1:T(8,128)(2,1)} %collective-permute-done.18), channel_id=1, source_target_pairs={{0,2},{2,4},{4,6},{6,8},{8,10},{10,12},{12,14},{14,0},{1,3},{3,5},... | collective-permute-start | bytes 6291464 | tf_op jit(solution)/shard_map/ppermute | solution.py:23
  753.2 89.9 %collective-permute-start.3 = (bf16[2048,512]{0,1:T(8,128)(2,1)}, bf16[2048,512]{0,1:T(8,128)(2,1)}, u32[]{:S(2)}, u32[]{:S(2)}) collective-permute-start(bf16[2048,512]{0,1:T(8,128)(2,1)} %collective-permute-done.2), channel_id=1, source_target_pairs={{0,2},{2,4},{4,6},{6,8},{8,10},{10,12},{12,14},{14,0},{1,3},{3,5},... | collective-permute-start | bytes 6291464 | tf_op jit(solution)/shard_map/ppermute | solution.py:23
  798.1 89.9 %collective-permute-start.20 = (bf16[2048,512]{0,1:T(8,128)(2,1)}, bf16[2048,512]{0,1:T(8,128)(2,1)}, u32[]{:S(2)}, u32[]{:S(2)}) collective-permute-start(bf16[2048,512]{0,1:T(8,128)(2,1)} %collective-permute-done.19), channel_id=1, source_target_pairs={{0,2},{2,4},{4,6},{6,8},{8,10},{10,12},{12,14},{14,0},{1,3},{3,5},... | collective-permute-start | bytes 6291464 | tf_op jit(solution)/shard_map/ppermute | solution.py:23
  798.1 103.6 %collective-permute-start.21 = (bf16[4096,512]{0,1:T(8,128)(2,1)}, bf16[4096,512]{0,1:T(8,128)(2,1)}, u32[]{:S(2)}, u32[]{:S(2)}) collective-permute-start(bf16[4096,512]{0,1:T(8,128)(2,1)} %all-gather.5.cloned.1.call-done), channel_id=1, source_target_pairs={{0,1},{2,3},{4,5},{6,7},{8,9},{10,11},{12,13},{14,15},{16,17},{18,... | collective-permute-start | bytes 12582920 | tf_op jit(solution)/shard_map/ppermute | solution.py:13
  843.1 84.0 %collective-permute-start.4 = (bf16[2048,512]{0,1:T(8,128)(2,1)}, bf16[2048,512]{0,1:T(8,128)(2,1)}, u32[]{:S(2)}, u32[]{:S(2)}) collective-permute-start(bf16[2048,512]{0,1:T(8,128)(2,1)} %collective-permute-done.3), channel_id=1, source_target_pairs={{0,2},{2,4},{4,6},{6,8},{8,10},{10,12},{12,14},{14,0},{1,3},{3,5},... | collective-permute-start | bytes 6291464 | tf_op jit(solution)/shard_map/ppermute | solution.py:23
  927.0 46.3 %collective-permute-start.5 = (bf16[2048,512]{0,1:T(8,128)(2,1)}, bf16[2048,512]{0,1:T(8,128)(2,1)}, u32[]{:S(2)}, u32[]{:S(2)}) collective-permute-start(bf16[2048,512]{0,1:T(8,128)(2,1)} %collective-permute-done.4), channel_id=1, source_target_pairs={{0,2},{2,4},{4,6},{6,8},{8,10},{10,12},{12,14},{14,0},{1,3},{3,5},... | collective-permute-start | bytes 6291464 | tf_op jit(solution)/shard_map/ppermute | solution.py:23
  973.3 69.3 %collective-permute-start.22 = (bf16[4096,512]{0,1:T(8,128)(2,1)}, bf16[4096,512]{0,1:T(8,128)(2,1)}, u32[]{:S(2)}, u32[]{:S(2)}) collective-permute-start(bf16[4096,512]{0,1:T(8,128)(2,1)} %all-gather.7.cloned.1.call-done), channel_id=1, source_target_pairs={{0,1},{2,3},{4,5},{6,7},{8,9},{10,11},{12,13},{14,15},{16,17},{18,... | collective-permute-start | bytes 12582920 | tf_op jit(solution)/shard_map/ppermute | solution.py:13
  (20 other events, 1145.3 us)
Sparse Core Ops, SparseCore 0:
  309.0 57.1 all-gather.8
  618.5 57.3 all-gather.4
  917.2 53.4 all-gather.6
